TPU v7x, 32 devices: a whole 2x2x4 slice. The times are simulated.
32 devices in a mesh: dp: 8 (over z, y), mp: 4 (over x, core).
Axes of the slice: x: 2, y: 2, z: 4, core: 2. Of those that a mesh axis runs over, the one named last changes fastest.
Arguments:
- tokens: bfloat16 [32, 256, 1152], P('dp'), may hold values from -6 to 6
- condition: bfloat16 [32, 1152], P('dp'), may hold values from -6 to 6
- cotangent: bfloat16 [32, 256, 1152], P('dp'), may hold values from -12 to 12
- kept_index: int32 [32, 128], P('dp'), may hold values from 0 to 255, as said below
- skip_index: int32 [32, 128], P('dp'), may hold values from 0 to 255, as said below
- step_count: int32 [1], replicated, may hold values from 1 to 20
- ada_weight: float32 [1152, 6, 1152], P('dp', None, 'mp'), may hold values from -0.1875 to 0.1875
- qkv_weight: float32 [3, 1152, 1152], P(None, 'dp', 'mp'), may hold values from -0.1875 to 0.1875
- proj_weight: float32 [1152, 1152], P('mp', 'dp'), may hold values from -1 to 1
- fc1_weight: float32 [1152, 4608], P('dp', 'mp'), may hold values from -0.1875 to 0.1875
- fc2_weight: float32 [4608, 1152], P('mp', 'dp'), may hold values from -0.09375 to 0.09375
- ada_moment: float32 [1152, 6, 1152], P('dp', None, 'mp'), may hold values from -80 to 80
- qkv_moment: float32 [3, 1152, 1152], P(None, 'dp', 'mp'), may hold values from -80 to 80
- proj_moment: float32 [1152, 1152], P('mp', 'dp'), may hold values from -80 to 80
- fc1_moment: float32 [1152, 4608], P('dp', 'mp'), may hold values from -80 to 80
- fc2_moment: float32 [4608, 1152], P('mp', 'dp'), may hold values from -80 to 80
- ada_average: float32 [1152, 6, 1152], P('dp', None, 'mp'), may hold values from -0.1875 to 0.1875
- qkv_average: float32 [3, 1152, 1152], P(None, 'dp', 'mp'), may hold values from -0.1875 to 0.1875
- proj_average: float32 [1152, 1152], P('mp', 'dp'), may hold values from -1 to 1
- fc1_average: float32 [1152, 4608], P('dp', 'mp'), may hold values from -0.1875 to 0.1875
- fc2_average: float32 [4608, 1152], P('mp', 'dp'), may hold values from -0.09375 to 0.09375
Outputs:
- block_out: bfloat16 [32, 256, 1152], P('dp')
- tokens_grad: float32 [32, 256, 1152], P('dp')
- condition_grad: float32 [32, 1152], P('dp')
- ada_master: float32 [1152, 6, 1152], P('dp', None, 'mp')
- qkv_master: float32 [3, 1152, 1152], P(None, 'dp', 'mp')
- proj_master: float32 [1152, 1152], P('mp', 'dp')
- fc1_master: float32 [1152, 4608], P('dp', 'mp')
- fc2_master: float32 [4608, 1152], P('mp', 'dp')
- ada_momentum: float32 [1152, 6, 1152], P('dp', None, 'mp')
- qkv_momentum: float32 [3, 1152, 1152], P(None, 'dp', 'mp')
- proj_momentum: float32 [1152, 1152], P('mp', 'dp')
- fc1_momentum: float32 [1152, 4608], P('dp', 'mp')
- fc2_momentum: float32 [4608, 1152], P('mp', 'dp')
- ada_ema: float32 [1152, 6, 1152], P('dp', None, 'mp')
- qkv_ema: float32 [3, 1152, 1152], P(None, 'dp', 'mp')
- proj_ema: float32 [1152, 1152], P('mp', 'dp')
- fc1_ema: float32 [1152, 4608], P('dp', 'mp')
- fc2_ema: float32 [4608, 1152], P('mp', 'dp')
Inputs may be any that keep to these rules, and one draw needn't show every extreme that they name: `kept_index`: row b lists 128 distinct positions of image b in increasing order; row b of skip_index lists the other 128 positions in increasing order. `skip_index`: row b lists the positions of image b that kept_index does not, in increasing order.
All inputs are finite; a program needn't handle non-finite values.
Results may differ from a plain program's by a relative error of at most 0.012.
The roundings to bfloat16 on the way count: a program that leaves them out, or rounds other values in their place, can miss the bound.
Values may be sent and summed in bfloat16 or wider, within the bound.
No kernel may reach another device: no remote copies, remote signals or barrier semaphores. Data moves between devices by JAX's collectives and lax.ppermute only.
A program may use at most 192 MiB of HBM per device.

v0:
```python
from functools import partial
import math
import jax
import jax.numpy as jnp
from jax import lax
from jax.sharding import PartitionSpec as P

HEAD_DIM = 72
epsilon = 1e-06
momentum_rate = 0.9


def layer_norm(values):
    centered = values - jnp.mean(values, axis=-1, keepdims=True)
    inverse = lax.rsqrt(jnp.mean(centered * centered, axis=-1, keepdims=True) + epsilon)
    return (centered * inverse, inverse)


def norm_back(normed, inverse, gradient):
    return inverse * (
        gradient
        - jnp.mean(gradient, axis=-1, keepdims=True)
        - normed * jnp.mean(gradient * normed, axis=-1, keepdims=True)
    )


def pick_rows(values, index):
    return jnp.take_along_axis(values, index[:, :, None], axis=1)


def place_rows(kept_rows, other_rows, kept_index, skip_index):
    images = kept_index.shape[0]
    batch = jnp.arange(images, dtype=jnp.int32)[:, None]
    blank = jnp.zeros(
        (images, kept_index.shape[1] + skip_index.shape[1], kept_rows.shape[2]), kept_rows.dtype
    )
    return blank.at[batch, kept_index].set(kept_rows).at[batch, skip_index].set(other_rows)


def share_rows(values):
    return lax.psum_scatter(values, "mp", scatter_dimension=1, tiled=True)


def whole_rows(values):
    return lax.all_gather(values, "mp", axis=1, tiled=True)


def per_device(
    tokens,
    condition,
    cotangent,
    kept_index,
    skip_index,
    step_count,
    ada_weight,
    qkv_weight,
    proj_weight,
    fc1_weight,
    fc2_weight,
    ada_moment,
    qkv_moment,
    proj_moment,
    fc1_moment,
    fc2_moment,
    ada_average,
    qkv_average,
    proj_average,
    fc1_average,
    fc2_average,
):
    f32 = jnp.float32
    bf16 = jnp.bfloat16
    ada_low = ada_weight.astype(bf16)
    qkv_low = qkv_weight.astype(bf16)
    proj_low = proj_weight.astype(bf16)
    fc1_low = fc1_weight.astype(bf16)
    fc2_low = fc2_weight.astype(bf16)
    ada_full, qkv_full, proj_full, fc1_full, fc2_full = (
        lax.all_gather(ada_low, "dp", axis=0, tiled=True),
        lax.all_gather(qkv_low, "dp", axis=1, tiled=True),
        lax.all_gather(proj_low, "dp", axis=1, tiled=True),
        lax.all_gather(fc1_low, "dp", axis=0, tiled=True),
        lax.all_gather(fc2_low, "dp", axis=1, tiled=True),
    )
    images = tokens.shape[0]
    kept_count = kept_index.shape[1]
    local_width = qkv_full.shape[2]
    local_heads = local_width // HEAD_DIM
    score_scale = HEAD_DIM ** (-0.5)
    row_share = kept_count // lax.axis_size("mp")
    row_start = lax.axis_index("mp") * row_share

    def own_rows(values):
        return lax.dynamic_slice_in_dim(values, row_start, row_share, 1)

    cond_float = condition.astype(f32)
    silu_cond = jax.nn.silu(cond_float).astype(bf16)
    mod_part = jnp.einsum("bd,dkf->bkf", silu_cond, ada_full, preferred_element_type=f32)
    modulation = lax.all_gather(mod_part, "mp", axis=2, tiled=True)
    shift_one = modulation[:, 0, None, :]
    scale_one = modulation[:, 1, None, :]
    gate_one = modulation[:, 2, None, :]
    shift_two = modulation[:, 3, None, :]
    scale_two = modulation[:, 4, None, :]
    gate_two = modulation[:, 5, None, :]
    kept_rows = pick_rows(tokens, kept_index).astype(f32)
    normed_one, inverse_one = layer_norm(kept_rows)
    hidden = (normed_one * (1.0 + scale_one) + shift_one).astype(bf16)
    projected = jnp.einsum("bnd,tdf->tbnf", hidden, qkv_full, preferred_element_type=f32).astype(
        bf16
    )
    split_heads = projected.reshape(3, images, kept_count, local_heads, HEAD_DIM)
    query_heads = split_heads[0]
    key_heads = split_heads[1]
    value_heads = split_heads[2]
    scores = (
        jnp.einsum("bqhe,bkhe->bhqk", query_heads, key_heads, preferred_element_type=f32)
        * score_scale
    )
    row_max = jnp.max(scores, axis=-1, keepdims=True)
    exp_scores = jnp.exp(scores - row_max)
    row_total = jnp.sum(exp_scores, axis=-1, keepdims=True)
    log_total = row_max + jnp.log(row_total)
    probs = exp_scores / row_total
    attended = (
        jnp.einsum("bhqk,bkhe->bqhe", probs.astype(bf16), value_heads, preferred_element_type=f32)
        .astype(bf16)
        .reshape(images, kept_count, local_width)
    )
    attn_part = jnp.einsum("bnf,fd->bnd", attended, proj_full, preferred_element_type=f32)
    attn_out = share_rows(attn_part)
    residual = own_rows(kept_rows) + gate_one * attn_out
    normed_two, inverse_two = layer_norm(residual)
    hidden_two = whole_rows((normed_two * (1.0 + scale_two) + shift_two).astype(bf16))
    pre_act = jnp.einsum("bnd,df->bnf", hidden_two, fc1_full, preferred_element_type=f32)
    activated = jax.nn.gelu(pre_act, approximate=True).astype(bf16)
    mlp_part = jnp.einsum("bnf,fd->bnd", activated, fc2_full, preferred_element_type=f32)
    mlp_out = share_rows(mlp_part)
    kept_out = residual + gate_two * mlp_out
    kept_low = whole_rows(kept_out.astype(bf16))
    block_out = place_rows(kept_low, pick_rows(tokens, skip_index), kept_index, skip_index)
    ada_back, qkv_back, proj_back, fc1_back, fc2_back = (
        lax.all_gather(ada_low, "dp", axis=0, tiled=True),
        lax.all_gather(qkv_low, "dp", axis=1, tiled=True),
        lax.all_gather(proj_low, "dp", axis=1, tiled=True),
        lax.all_gather(fc1_low, "dp", axis=0, tiled=True),
        lax.all_gather(fc2_low, "dp", axis=1, tiled=True),
    )
    grad_float = cotangent.astype(f32)
    grad_kept = pick_rows(grad_float, kept_index)
    grad_here = own_rows(grad_kept)
    gate_two_grad = jnp.sum(grad_here * mlp_out, axis=1)
    mlp_out_grad = (gate_two * grad_kept).astype(bf16)
    fc2_grad = jnp.einsum("bnf,bnd->fd", activated, mlp_out_grad, preferred_element_type=f32)
    act_grad = jnp.einsum("bnd,fd->bnf", mlp_out_grad, fc2_back, preferred_element_type=f32)
    gelu_value, gelu_pull = jax.vjp(partial(jax.nn.gelu, approximate=True), pre_act)
    pre_grad = gelu_pull(act_grad)[0].astype(bf16)
    fc1_grad = jnp.einsum("bnd,bnf->df", hidden_two, pre_grad, preferred_element_type=f32)
    hidden_two_part = jnp.einsum("bnf,df->bnd", pre_grad, fc1_back, preferred_element_type=f32)
    hidden_two_grad = share_rows(hidden_two_part)
    shift_two_grad = jnp.sum(hidden_two_grad, axis=1)
    scale_two_grad = jnp.sum(hidden_two_grad * normed_two, axis=1)
    residual_grad = grad_here + norm_back(
        normed_two, inverse_two, hidden_two_grad * (1.0 + scale_two)
    )
    gate_one_grad = jnp.sum(residual_grad * attn_out, axis=1)
    attn_out_grad = whole_rows((gate_one * residual_grad).astype(bf16))
    proj_grad = jnp.einsum("bnf,bnd->fd", attended, attn_out_grad, preferred_element_type=f32)
    attended_grad = jnp.einsum(
        "bnd,fd->bnf", attn_out_grad, proj_back, preferred_element_type=f32
    ).astype(bf16)
    attended_grad = attended_grad.reshape(images, kept_count, local_heads, HEAD_DIM)
    again_scores = (
        jnp.einsum("bqhe,bkhe->bhqk", query_heads, key_heads, preferred_element_type=f32)
        * score_scale
    )
    again_probs = jnp.exp(again_scores - log_total)
    prob_grad = jnp.einsum(
        "bqhe,bkhe->bhqk", attended_grad, value_heads, preferred_element_type=f32
    )
    score_grad = (
        again_probs * (prob_grad - jnp.sum(prob_grad * again_probs, axis=-1, keepdims=True))
    ).astype(bf16)
    query_grad = (
        jnp.einsum("bhqk,bkhe->bqhe", score_grad, key_heads, preferred_element_type=f32)
        * score_scale
    )
    key_grad = (
        jnp.einsum("bhqk,bqhe->bkhe", score_grad, query_heads, preferred_element_type=f32)
        * score_scale
    )
    value_grad = jnp.einsum(
        "bhqk,bqhe->bkhe", again_probs.astype(bf16), attended_grad, preferred_element_type=f32
    )
    grad_rows = (
        jnp.stack([query_grad, key_grad, value_grad])
        .astype(bf16)
        .reshape(3, images, kept_count, local_width)
    )
    qkv_grad = jnp.einsum("tbnf,bnd->tdf", grad_rows, hidden, preferred_element_type=f32)
    hidden_part = jnp.einsum("tbnf,tdf->bnd", grad_rows, qkv_back, preferred_element_type=f32)
    hidden_grad = share_rows(hidden_part)
    normed_here = own_rows(normed_one)
    inverse_here = own_rows(inverse_one)
    shift_one_grad = jnp.sum(hidden_grad, axis=1)
    scale_one_grad = jnp.sum(hidden_grad * normed_here, axis=1)
    kept_share = residual_grad + norm_back(
        normed_here, inverse_here, hidden_grad * (1.0 + scale_one)
    )
    kept_grad = lax.all_gather(kept_share, "mp", axis=1, tiled=True)
    tokens_grad = place_rows(kept_grad, pick_rows(grad_float, skip_index), kept_index, skip_index)
    mod_grad = jnp.stack(
        [
            shift_one_grad,
            scale_one_grad,
            gate_one_grad,
            shift_two_grad,
            scale_two_grad,
            gate_two_grad,
        ],
        axis=1,
    )
    mod_local = lax.psum_scatter(mod_grad, "mp", scatter_dimension=2, tiled=True).astype(bf16)
    ada_grad = jnp.einsum("bd,bkf->dkf", silu_cond, mod_local, preferred_element_type=f32)
    silu_grad = lax.psum(
        jnp.einsum("bkf,dkf->bd", mod_local, ada_back, preferred_element_type=f32), "mp"
    )
    silu_value, silu_pull = jax.vjp(jax.nn.silu, cond_float)
    condition_grad = silu_pull(silu_grad)[0]
    ada_shard, qkv_shard, proj_shard, fc1_shard, fc2_shard = (
        lax.psum_scatter(ada_grad, "dp", scatter_dimension=0, tiled=True),
        lax.psum_scatter(qkv_grad, "dp", scatter_dimension=1, tiled=True),
        lax.psum_scatter(proj_grad, "dp", scatter_dimension=1, tiled=True),
        lax.psum_scatter(fc1_grad, "dp", scatter_dimension=0, tiled=True),
        lax.psum_scatter(fc2_grad, "dp", scatter_dimension=1, tiled=True),
    )
    rate = 0.02 / math.sqrt(images * lax.axis_size("dp") * kept_count)
    step_float = step_count.astype(f32)[0]
    decay = (1.0 + step_float) / (10.0 + step_float)

    def update(weight, moment, average, gradient):
        new_moment = momentum_rate * moment + gradient
        master = weight - rate * (gradient + momentum_rate * new_moment)
        return (master, new_moment, decay * average + (1.0 - decay) * master)

    ada_master, ada_momentum, ada_ema = update(ada_weight, ada_moment, ada_average, ada_shard)
    qkv_master, qkv_momentum, qkv_ema = update(qkv_weight, qkv_moment, qkv_average, qkv_shard)
    proj_master, proj_momentum, proj_ema = update(
        proj_weight, proj_moment, proj_average, proj_shard
    )
    fc1_master, fc1_momentum, fc1_ema = update(fc1_weight, fc1_moment, fc1_average, fc1_shard)
    fc2_master, fc2_momentum, fc2_ema = update(fc2_weight, fc2_moment, fc2_average, fc2_shard)
    return (
        block_out,
        tokens_grad,
        condition_grad,
        ada_master,
        qkv_master,
        proj_master,
        fc1_master,
        fc2_master,
        ada_momentum,
        qkv_momentum,
        proj_momentum,
        fc1_momentum,
        fc2_momentum,
        ada_ema,
        qkv_ema,
        proj_ema,
        fc1_ema,
        fc2_ema,
    )


def solution(mesh):
    placed = (
        P("dp", None, None),
        P("dp", None),
        P("dp", None, None),
        P("dp", None),
        P("dp", None),
        P(),
        P("dp", None, "mp"),
        P(None, "dp", "mp"),
        P("mp", "dp"),
        P("dp", "mp"),
        P("mp", "dp"),
        P("dp", None, "mp"),
        P(None, "dp", "mp"),
        P("mp", "dp"),
        P("dp", "mp"),
        P("mp", "dp"),
        P("dp", None, "mp"),
        P(None, "dp", "mp"),
        P("mp", "dp"),
        P("dp", "mp"),
        P("mp", "dp"),
    )
    return jax.shard_map(
        per_device,
        mesh=mesh,
        in_specs=placed,
        out_specs=(
            P("dp", None, None),
            P("dp", None, None),
            P("dp", None),
            P("dp", None, "mp"),
            P(None, "dp", "mp"),
            P("mp", "dp"),
            P("dp", "mp"),
            P("mp", "dp"),
            P("dp", None, "mp"),
            P(None, "dp", "mp"),
            P("mp", "dp"),
            P("dp", "mp"),
            P("mp", "dp"),
            P("dp", None, "mp"),
            P(None, "dp", "mp"),
            P("mp", "dp"),
            P("dp", "mp"),
            P("mp", "dp"),
        ),
        check_vma=False,
    )
```

profile of v0, /device:TPU:0, one launch (start us, length us, event | category | flops | bytes accessed | tf_op | source)
XLA Modules:
  0.0 1142.5 jit_solution(12994166128726137092)
XLA Ops:
  11.3 5.7 gather_fusion
  18.1 38.6 %all_gather.38 = bf16[288,1152]{0,1:T(8,128)(2,1)} all-gather(bf16[288,144]{0,1:T(8,128)(2,1)S(1)} %copy-done.21), channel_id=1, replica_groups=mesh['dp'=8,'mp'=4] {'dp'}, dimensions={1}, use_global_device_ids=true | all-gather | bytes 746496 | tf_op jit(solution)/shard_map/all_gather | solution.py:81
  56.7 51.9 %all-gather.9.cloned.1.call-done = bf16[1152,6,288]{2,0,1:T(8,128)(2,1)} async-done(((bf16[144,6,288]{2,0,1:T(8,128)(2,1)}), bf16[1152,6,288]{2,0,1:T(8,128)(2,1)}) %all-gather.9.cloned.1.call-update) | async-done | bytes 3981328 | tf_op jit(solution)/shard_map/all_gather | solution.py:79
  108.6 3.9 fusion.50
  114.4 17.3 %all_gather.36 = f32[4,6,1152]{1,0,2:T(4,128)S(1)} all-gather(f32[4,6,288]{1,0,2:T(4,128)} %copy.115), channel_id=1, replica_groups=mesh['dp'=8,'mp'=4] {'mp'}, dimensions={2}, use_global_device_ids=true | all-gather | bytes 138240 | tf_op jit(solution)/shard_map/all_gather | solution.py:99
  131.7 9.2 fusion.74
  147.7 17.1 %all-gather.11.cloned.1.call-done = bf16[3,1152,288]{2,1,0:T(8,128)(2,1)} async-done(((bf16[3,144,288]{2,1,0:T(8,128)(2,1)}), bf16[3,1152,288]{2,1,0:T(8,128)(2,1)}) %all-gather.11.cloned.1.call-update) | async-done | bytes 1990672 | tf_op jit(solution)/shard_map/all_gather | solution.py:80
  164.7 3.6 fusion.23
  186.2 18.3 %reduce-scatter.15.cloned.1.call-done = f32[4,32,1152]{2,1,0:T(8,128)} async-done(((f32[4,128,1152]{2,1,0:T(8,128)}), f32[4,32,1152]{2,1,0:T(8,128)}) %reduce-scatter.15.cloned.1.call-update) | async-done | bytes 589840 | tf_op jit(solution)/shard_map/reduce_scatter | solution.py:41
  207.8 4.2 convert_element_type.97
  212.0 11.0 gather_fusion.2
  222.9 4.3 subtract_multiply_fusion
  230.0 32.5 %all-gather.15.cloned.1.call-done = bf16[1152,1152]{1,0:T(8,128)(2,1)} async-done(((bf16[144,1152]{1,0:T(8,128)(2,1)}), bf16[1152,1152]{1,0:T(8,128)(2,1)}) %all-gather.15.cloned.1.call-update) | async-done | bytes 2654224 | tf_op jit(solution)/shard_map/all_gather | solution.py:82
  262.5 18.1 %all-gather.13.cloned.1.call-done = bf16[4,128,1152]{2,1,0:T(8,128)(2,1)} async-done(((bf16[4,32,1152]{2,1,0:T(8,128)(2,1)}), bf16[4,128,1152]{2,1,0:T(8,128)(2,1)}) %all-gather.13.cloned.1.call-update) | async-done | bytes 1179664 | tf_op jit(solution)/shard_map/all_gather | solution.py:45
  280.6 4.1 fusion.6
  286.1 4.3 convolution_bitcast_fusion
  291.1 103.6 %reduce-scatter.29.cloned.1.call-done = f32[1152,144]{0,1:T(8,128)} async-done(((f32[1152,1152]{0,1:T(8,128)}), f32[1152,144]{0,1:T(8,128)}) %reduce-scatter.29.cloned.1.call-update) | async-done | bytes 663568 | tf_op jit(solution)/shard_map/reduce_scatter | solution.py:235
  394.7 3.4 multiply_add_fusion.4
  398.2 54.9 %all-gather.17.cloned.1.call-done = bf16[1152,1152]{0,1:T(8,128)(2,1)} async-done(((bf16[1152,144]{0,1:T(8,128)(2,1)}), bf16[1152,1152]{0,1:T(8,128)(2,1)}) %all-gather.17.cloned.1.call-update) | async-done | bytes 2654224 | tf_op jit(solution)/shard_map/all_gather | solution.py:83
  453.1 5.8 fusion.17
  459.9 3.4 fusion.4
  463.6 6.1 fusion.2
  469.7 25.4 %reduce-scatter.19.cloned.1.call-done = f32[4,32,1152]{2,1,0:T(8,128)} async-done(((f32[4,128,1152]{2,1,0:T(8,128)}), f32[4,32,1152]{2,1,0:T(8,128)}) %reduce-scatter.19.cloned.1.call-update) | async-done | bytes 589840 | tf_op jit(solution)/shard_map/reduce_scatter | solution.py:41
  497.9 33.0 %reduce-scatter.17.cloned.1.call-done = f32[4,32,1152]{2,1,0:T(8,128)} async-done(((f32[4,128,1152]{2,1,0:T(8,128)}), f32[4,32,1152]{2,1,0:T(8,128)}) %reduce-scatter.17.cloned.1.call-update) | async-done | bytes 589840 | tf_op jit(solution)/shard_map/reduce_scatter | solution.py:41
  531.0 3.5 multiply_reduce_fusion.4
  536.8 16.8 %all-gather.21.cloned.1.call-done = bf16[4,128,1152]{2,1,0:T(8,128)(2,1)} async-done(((bf16[4,32,1152]{2,1,0:T(8,128)(2,1)}), bf16[4,128,1152]{2,1,0:T(8,128)(2,1)}) %all-gather.21.cloned.1.call-update) | async-done | bytes 1179664 | tf_op jit(solution)/shard_map/all_gather | solution.py:45
  562.4 33.2 %reduce-scatter.21.cloned.1.call-done = f32[4,32,1152]{2,1,0:T(8,128)} async-done(((f32[4,128,1152]{2,1,0:T(8,128)}), f32[4,32,1152]{2,1,0:T(8,128)}) %reduce-scatter.21.cloned.1.call-update) | async-done | bytes 589840 | tf_op jit(solution)/shard_map/reduce_scatter | solution.py:41
  604.3 3.8 copy.145
  608.0 4.1 reshape.212
  613.0 3.4 convolution_bitcast_fusion.4
  616.5 5.8 convolution_bitcast_fusion.1
  622.9 4.7 convolution_bitcast_fusion.2
  627.6 8.6 copy.147
  636.2 9.0 reshape.214
  651.3 5.7 fusion.46
  658.4 11.0 gather_fusion.3
  669.4 8.4 gather_fusion.1
  688.4 78.5 %scatter_fusion = bf16[4,256,1152]{2,1,0:T(8,128)(2,1)} fusion(bf16[4,256,1152]{2,1,0:T(8,128)(2,1)} %broadcast_in_dim.28, s32[512]{0:T(512)S(1)} %get-tuple-element.152, bf16[512,1152]{1,0:T(8,128)(2,1)} %bitcast.198), kind=kCustom, calls=%fused_computation.4 | custom fusion | bytes 3543040 | tf_op jit(solution)/shard_map/scatter | solution.py:37
  766.9 78.8 %scatter_fusion.1 = bf16[4,256,1152]{2,1,0:T(8,128)(2,1)} fusion(bf16[4,256,1152]{2,1,0:T(8,128)(2,1)} %scatter_fusion, s32[512]{0:T(512)S(1)} %get-tuple-element.150, bf16[512,1152]{1,0:T(8,128)(2,1)} %bitcast.187), kind=kCustom, calls=%fused_computation.5 | custom fusion | bytes 3543040 | tf_op jit(solution)/shard_map/scatter | solution.py:37
  850.9 4.0 convolution_bitcast_fusion.5
  854.9 11.2 psum.7
  866.8 55.1 %reduce-scatter.33.cloned.1.call-done = f32[144,864]{1,0:T(8,128)} async-done(((f32[1152,864]{1,0:T(8,128)}), f32[144,864]{1,0:T(8,128)}) %reduce-scatter.33.cloned.1.call-update) | async-done | bytes 497680
  926.7 3.5 multiply_add_fusion.2
  936.3 10.9 all-gather.23.cloned.1.call-done
  949.7 80.0 %scatter_fusion.2 = f32[4,256,1152]{2,1,0:T(8,128)} fusion(f32[4,256,1152]{2,1,0:T(8,128)} %broadcast_in_dim.35, s32[512]{0:T(512)S(1)} %get-tuple-element.152, f32[512,1152]{1,0:T(8,128)} %bitcast.196), kind=kCustom, calls=%fused_computation.6 | custom fusion | bytes 7081984 | tf_op jit(solution)/shard_map/scatter | solution.py:37
  1029.7 79.8 %scatter_fusion.3 = f32[4,256,1152]{2,1,0:T(8,128)} fusion(f32[4,256,1152]{2,1,0:T(8,128)} %scatter_fusion.2, s32[512]{0:T(512)S(1)} %get-tuple-element.150, f32[512,1152]{1,0:T(8,128)} %bitcast.184), kind=kCustom, calls=%fused_computation.7 | custom fusion | bytes 7081984 | tf_op jit(solution)/shard_map/scatter | solution.py:37
  1109.5 21.1 %reduce-scatter.23.cloned.1.call-done = f32[144,6,288]{2,0,1:T(8,128)} async-done(((f32[1152,6,288]{2,0,1:T(8,128)}), f32[144,6,288]{2,0,1:T(8,128)}) %reduce-scatter.23.cloned.1.call-update) | async-done | bytes 995344 | tf_op jit(solution)/shard_map/reduce_scatter | solution.py:231
  1130.6 4.8 multiply_add_fusion
  (201 shorter events, 101.5 us)
Async XLA Ops:
  7.2 4.1 copy-start
  7.2 2.5 copy-start.14
  7.2 3.4 copy-start.19
  7.2 4.0 copy-start.39
  7.2 101.4 %all-gather.9.cloned.1.call-start = ((), (), s32[]{:S(2)}) async-start(), calls=%async_computation.10 | async-start | bytes 5971968 | tf_op jit(solution)/shard_map/all_gather | solution.py:79
  9.7 155.0 %all-gather.11.cloned.1.call-start = ((), (), s32[]{:S(2)}) async-start(), calls=%async_computation.11 | async-start | bytes 2985984 | tf_op jit(solution)/shard_map/all_gather | solution.py:80
  10.5 194.0 %reduce-scatter.15.cloned.1.call-start = ((), (), s32[]{:S(2)}) async-start(), calls=%async_computation.12 | async-start | bytes 2949120 | tf_op jit(solution)/shard_map/reduce_scatter | solution.py:41
  17.0 1.1 copy-start.21
  17.5 147.2 %copy-start.32 = (f32[4,128]{1,0:T(4,128)}, f32[4,128]{1,0:T(4,128)S(1)}, u32[]{:S(2)}) copy-start(f32[4,128]{1,0:T(4,128)S(1)} %broadcast_multiply_fusion.5) | copy-start | bytes 6148
  18.1 146.7 %copy-start.34 = (f32[4,128]{1,0:T(4,128)}, f32[4,128]{1,0:T(4,128)S(1)}, u32[]{:S(2)}) copy-start(f32[4,128]{1,0:T(4,128)S(1)} %add_rsqrt_fusion.1) | copy-start | bytes 6148
  168.4 1.2 copy-start.10
  168.4 1.2 copy-start.17
  169.3 1.2 copy-start.5
  172.8 2.2 copy-start.37
  172.8 89.7 %all-gather.15.cloned.1.call-start = ((), (), s32[]{:S(2)}) async-start(), calls=%async_computation.14 | async-start | bytes 2985984 | tf_op jit(solution)/shard_map/all_gather | solution.py:82
  174.7 105.9 %all-gather.13.cloned.1.call-start = ((), (), s32[]{:S(2)}) async-start(), calls=%async_computation.13 | async-start | bytes 1474560 | tf_op jit(solution)/shard_map/all_gather | solution.py:45
  204.6 2.3 copy-start.25
  204.6 2.3 copy-start.30
  207.8 186.9 %reduce-scatter.29.cloned.1.call-start = ((), (), s32[]{:S(2)}) async-start(), calls=%async_computation.25 | async-start | bytes 5971968 | tf_op jit(solution)/shard_map/reduce_scatter | solution.py:235
  280.6 5.5 copy-start.8
  280.6 5.5 copy-start.29
  284.7 1.4 copy-start.43
  290.4 162.7 %all-gather.17.cloned.1.call-start = ((), (), s32[]{:S(2)}) async-start(), calls=%async_computation.15 | async-start | bytes 2985984 | tf_op jit(solution)/shard_map/all_gather | solution.py:83
  398.2 97.0 %reduce-scatter.19.cloned.1.call-start = ((), (), s32[]{:S(2)}) async-start(), calls=%async_computation.18 | async-start | bytes 2949120 | tf_op jit(solution)/shard_map/reduce_scatter | solution.py:41
  453.1 6.8 copy-start.42
  458.9 1.0 copy-start.44
  463.3 67.6 %reduce-scatter.17.cloned.1.call-start = ((), (), s32[]{:S(2)}) async-start(), calls=%async_computation.16 | async-start | bytes 2949120 | tf_op jit(solution)/shard_map/reduce_scatter | solution.py:41
  469.7 83.9 %all-gather.21.cloned.1.call-start = ((), (), s32[]{:S(2)}) async-start(), calls=%async_computation.19 | async-start | bytes 1474560 | tf_op jit(solution)/shard_map/all_gather | solution.py:45
  530.9 4.3 copy-start.26
  536.0 59.6 %reduce-scatter.21.cloned.1.call-start = ((), (), s32[]{:S(2)}) async-start(), calls=%async_computation.20 | async-start | bytes 2949120 | tf_op jit(solution)/shard_map/reduce_scatter | solution.py:41
  553.6 2.2 copy-start.2
  553.6 2.2 copy-start.18
  556.9 2.1 copy-start.41
  557.3 1.0 copy-start.23
  562.4 87.2 %reduce-scatter.31.cloned.1.call-start = ((), (), s32[]{:S(2)}) async-start(), calls=%async_computation.26 | async-start | bytes 737280
  612.2 74.7 %all-gather.19.cloned.1.call-start = ((), (), s32[]{:S(2)}) async-start(), calls=%async_computation.17 | async-start | bytes 1474560 | tf_op jit(solution)/shard_map/all_gather | solution.py:45
  612.9 232.7 %reduce-scatter.25.cloned.1.call-start = ((), (), s32[]{:S(2)}) async-start(), calls=%async_computation.23 | async-start | bytes 1990656 | tf_op jit(solution)/shard_map/reduce_scatter | solution.py:233
  616.4 231.3 %reduce-scatter.27.cloned.1.call-start = ((), (), s32[]{:S(2)}) async-start(), calls=%async_computation.24 | async-start | bytes 5971968 | tf_op jit(solution)/shard_map/reduce_scatter | solution.py:234
  622.3 299.6 %reduce-scatter.33.cloned.1.call-start = ((), (), s32[]{:S(2)}) async-start(), calls=%async_computation.27 | async-start | bytes 4644864
  645.2 2.2 copy-start.7
  645.2 2.2 copy-start.15
  645.2 6.0 copy-start.27
  645.2 302.0 %all-gather.23.cloned.1.call-start = ((), (), s32[]{:S(2)}) async-start(), calls=%async_computation.21 | async-start | bytes 2949120 | tf_op jit(solution)/shard_map/all_gather | solution.py:210
  649.6 481.1 %reduce-scatter.23.cloned.1.call-start = ((), (), s32[]{:S(2)}) async-start(), calls=%async_computation.22 | async-start | bytes 11943936 | tf_op jit(solution)/shard_map/reduce_scatter | solution.py:231
  656.9 1.5 copy-start.40
  682.5 2.7 copy-start.4
  766.9 78.8 %copy-start.20 = (f32[288,144]{0,1:T(8,128)S(1)}, f32[288,144]{0,1:T(8,128)}, u32[]{:S(2)}) copy-start(f32[288,144]{0,1:T(8,128)} %param.33) | copy-start | bytes 497668
  930.2 4.9 copy-start.9
  (15 other events, 11.3 us)
Sparse Core Ops, SparseCore 0:
  10.9 97.7 all-gather.8
  111.5 53.2 all-gather.10
  172.9 31.5 reduce-scatter.14
  207.4 55.0 all-gather.14
  264.5 16.0 all-gather.12
  290.5 104.1 reduce-scatter.28
  398.3 54.7 all-gather.16
  463.4 31.6 reduce-scatter.18
  497.8 33.0 reduce-scatter.16
  536.1 17.4 all-gather.20
  562.5 33.0 reduce-scatter.20
  612.3 22.0 reduce-scatter.30
  636.6 17.4 all-gather.18
  657.8 66.3 reduce-scatter.24
  727.6 102.9 reduce-scatter.26
  834.5 87.4 reduce-scatter.32
  923.3 23.8 all-gather.22
  950.6 179.9 reduce-scatter.22
where the time goes:
time: 1160 us; the launch traced here: 1140 us
  waiting for transfers between devices  493 us (42%)
  local copies, waits for them, and re-layouts  442 us (38%)
  blocking collectives  67.2 us (6%)
  matrix products  65 us (6%)
  other arithmetic  57.6 us (5%)
  between operations  15.7 us (1%)
    scatter x4, local copies, waits for them, and re-layouts, place_rows(): blank.at[batch, kept_index].set(kept_rows).at[batch, skip_index]  317 us
    reduce_scatter x4, waiting for transfers between devices, share_rows(): return lax.psum_scatter(values, 'mp', scatter_dimension=1, tiled=True)  110 us
    reduce_scatter x1, waiting for transfers between devices, per_device(): lax.psum_scatter(fc2_grad, 'dp', scatter_dimension=1, tiled=True)  104 us
    unnamed x111, local copies, waits for them, and re-layouts  61.3 us
    unnamed x20, waiting for transfers between devices  56.1 us
    all_gather x1, waiting for transfers between devices, per_device(): lax.all_gather(fc2_low, 'dp', axis=1, tiled=True)  54.9 us
    all_gather x1, waiting for transfers between devices, per_device(): lax.all_gather(ada_low, 'dp', axis=0, tiled=True)  51.9 us
    all_gather x1, blocking collectives, per_device(): lax.all_gather(proj_low, 'dp', axis=1, tiled=True)  38.6 us
  transfers between devices with their start and end apart: 18, of which 14 were waited for; matrix products, arithmetic and copies ran while one was open for 43% of the time, Pallas kernels for 0%

commit v1 on v0

--- a/solution.py
+++ b/solution.py
@@ -8,6 +8,28 @@
 HEAD_DIM = 72
 epsilon = 1e-06
 momentum_rate = 0.9
+
+
+def laid_out(tiles, dim):
+    shape = list(tiles.shape[1:])
+    shape[dim] *= tiles.shape[0]
+    return jnp.moveaxis(tiles, 0, dim).reshape(shape)
+
+
+def gather_around(shard, axis, dim):
+    devices = lax.axis_size(axis)
+    pairs = [(i, (i + 1) % devices) for i in range(devices)]
+    back = [(b, a) for a, b in pairs]
+    lower, upper = ([], [])
+    for step in range(devices - 1):
+        if step % 2 == 0:
+            lower.append(lax.ppermute(lower[-1] if lower else shard, axis, pairs))
+        else:
+            upper.append(lax.ppermute(upper[-1] if upper else shard, axis, back))
+    blocks = jnp.stack([*lower[::-1], shard, *upper])
+    shift = lax.axis_index(axis) - len(lower)
+    blocks = blocks[(jnp.arange(devices) - shift) % devices]
+    return laid_out(blocks, dim)
 
 
 def layer_norm(values):
@@ -79,7 +101,7 @@
         lax.all_gather(ada_low, "dp", axis=0, tiled=True),
         lax.all_gather(qkv_low, "dp", axis=1, tiled=True),
         lax.all_gather(proj_low, "dp", axis=1, tiled=True),
-        lax.all_gather(fc1_low, "dp", axis=0, tiled=True),
+        gather_around(fc1_low, "dp", 0),
         lax.all_gather(fc2_low, "dp", axis=1, tiled=True),
     )
     images = tokens.shape[0]

time: 1160 us -> 1210 us (1.043)
  local copies, waits for them, and re-layouts: 442 us -> 458 us
  starting transfers between devices: 1.53 us -> 15.5 us
    ppermute x0 -> x7, waiting for transfers between devices: none -> 25.2 us  [the longest x4 24.2 us: gather_around(): lower.append(lax.ppermute(lower[-1] if lower else shard, axis, pairs))]
    reduce_scatter x4, waiting for transfers between devices: 110 us -> 91.5 us  [share_rows(): return lax.psum_scatter(values, 'mp', scatter_dimension=1, tiled=True)]
    all_gather x1, waiting for transfers between devices: 32.5 us -> 49.7 us  [per_device(): lax.all_gather(fc1_low, 'dp', axis=0, tiled=True)]
    all_gather x3, waiting for transfers between devices: 35 us -> 19.3 us  [whole_rows(): return lax.all_gather(values, 'mp', axis=1, tiled=True)]
    ppermute x0 -> x7, starting transfers between devices: none -> 13.8 us  [the longest x3 10.8 us: gather_around(): upper.append(lax.ppermute(upper[-1] if upper else shard, axis, back))]
    unnamed x111 -> x125, local copies, waits for them, and re-layouts: 61.3 us -> 70.9 us
  transfers between devices with their start and end apart: 18 -> 25, of which waited for: 14 -> 17; matrix products, arithmetic and copies ran while one was open for 43% -> 44% of each run, Pallas kernels for 0% -> 0%
where the time goes in v1:
time: 1210 us; the launch traced here: 1190 us
  waiting for transfers between devices  501 us (41%)
  local copies, waits for them, and re-layouts  458 us (38%)
  matrix products  67.9 us (6%)
  blocking collectives  67.3 us (6%)
  other arithmetic  59.8 us (5%)
  between operations  15.7 us (1%)
  starting transfers between devices  15.5 us (1%)
    scatter x4, local copies, waits for them, and re-layouts, place_rows(): blank.at[batch, kept_index].set(kept_rows).at[batch, skip_index]  317 us
    reduce_scatter x1, waiting for transfers between devices, per_device(): lax.psum_scatter(fc2_grad, 'dp', scatter_dimension=1, tiled=True)  104 us
    reduce_scatter x4, waiting for transfers between devices, share_rows(): return lax.psum_scatter(values, 'mp', scatter_dimension=1, tiled=True)  91.5 us
    unnamed x125, local copies, waits for them, and re-layouts  70.9 us
    unnamed x20, waiting for transfers between devices  56.9 us
    all_gather x1, waiting for transfers between devices, per_device(): lax.all_gather(fc2_low, 'dp', axis=1, tiled=True)  53.9 us
    all_gather x1, waiting for transfers between devices, per_device(): lax.all_gather(ada_low, 'dp', axis=0, tiled=True)  51.9 us
    all_gather x1, waiting for transfers between devices, per_device(): lax.all_gather(fc1_low, 'dp', axis=0, tiled=True)  49.7 us
  transfers between devices with their start and end apart: 25, of which 17 were waited for; matrix products, arithmetic and copies ran while one was open for 44% of the time, Pallas kernels for 0%

profile of v1, /device:TPU:0, one launch (start us, length us, event | category | flops | bytes accessed | tf_op | source)
XLA Modules:
  0.0 1185.5 jit_solution(16585765767043949789)
XLA Ops:
  11.3 5.7 gather_fusion.1
  18.1 38.6 %all_gather.37 = bf16[288,1152]{0,1:T(8,128)(2,1)} all-gather(bf16[288,144]{0,1:T(8,128)(2,1)S(1)} %copy-done.25), channel_id=1, replica_groups=mesh['dp'=8,'mp'=4] {'dp'}, dimensions={1}, use_global_device_ids=true | all-gather | bytes 746496 | tf_op jit(solution)/shard_map/all_gather | solution.py:103
  56.7 51.9 %all-gather.9.cloned.1.call-done = bf16[1152,6,288]{2,0,1:T(8,128)(2,1)} async-done(((bf16[144,6,288]{2,0,1:T(8,128)(2,1)}), bf16[1152,6,288]{2,0,1:T(8,128)(2,1)}) %all-gather.9.cloned.1.call-update) | async-done | bytes 3981328 | tf_op jit(solution)/shard_map/all_gather | solution.py:101
  108.6 3.9 fusion.48
  114.4 17.3 %all_gather.35 = f32[4,6,1152]{1,0,2:T(4,128)S(1)} all-gather(f32[4,6,288]{1,0,2:T(4,128)} %copy.115), channel_id=1, replica_groups=mesh['dp'=8,'mp'=4] {'mp'}, dimensions={2}, use_global_device_ids=true | all-gather | bytes 138240 | tf_op jit(solution)/shard_map/all_gather | solution.py:121
  131.7 9.2 fusion.74
  147.6 17.1 %all-gather.11.cloned.1.call-done = bf16[3,1152,288]{2,1,0:T(8,128)(2,1)} async-done(((bf16[3,144,288]{2,1,0:T(8,128)(2,1)}), bf16[3,1152,288]{2,1,0:T(8,128)(2,1)}) %all-gather.11.cloned.1.call-update) | async-done | bytes 1990672 | tf_op jit(solution)/shard_map/all_gather | solution.py:102
  164.7 3.6 fusion.21
  175.3 10.7 collective-permute-done
  186.0 4.9 collective-permute-start.4
  190.9 4.2 convert_element_type.97
  195.0 11.1 gather_fusion.3
  206.1 4.3 subtract_multiply_fusion
  210.4 4.7 collective-permute-start.5
  215.1 5.9 collective-permute-done.2
  228.1 7.5 collective-permute-done.3
  262.4 4.2 gather_fusion
  271.8 4.1 fusion.77
  277.3 4.2 convolution_bitcast_fusion
  282.3 103.6 %reduce-scatter.29.cloned.1.call-done = f32[1152,144]{0,1:T(8,128)} async-done(((f32[1152,1152]{0,1:T(8,128)}), f32[1152,144]{0,1:T(8,128)}) %reduce-scatter.29.cloned.1.call-update) | async-done | bytes 663568 | tf_op jit(solution)/shard_map/reduce_scatter | solution.py:257
  390.4 53.9 %all-gather.15.cloned.1.call-done = bf16[1152,1152]{0,1:T(8,128)(2,1)} async-done(((bf16[1152,144]{0,1:T(8,128)(2,1)}), bf16[1152,1152]{0,1:T(8,128)(2,1)}) %all-gather.15.cloned.1.call-update) | async-done | bytes 2654224 | tf_op jit(solution)/shard_map/all_gather | solution.py:105
  444.3 6.7 fusion.15
  451.0 49.7 %all-gather.19.cloned.1.call-done = bf16[1152,1152]{1,0:T(8,128)(2,1)} async-done(((bf16[144,1152]{1,0:T(8,128)(2,1)}), bf16[1152,1152]{1,0:T(8,128)(2,1)}) %all-gather.19.cloned.1.call-update) | async-done | bytes 2654224 | tf_op jit(solution)/shard_map/all_gather | solution.py:168
  500.7 5.4 fusion
  506.2 6.1 fusion.4
  512.3 25.6 %reduce-scatter.19.cloned.1.call-done = f32[4,32,1152]{2,1,0:T(8,128)} async-done(((f32[4,128,1152]{2,1,0:T(8,128)}), f32[4,32,1152]{2,1,0:T(8,128)}) %reduce-scatter.19.cloned.1.call-update) | async-done | bytes 589840 | tf_op jit(solution)/shard_map/reduce_scatter | solution.py:63
  540.7 33.0 %reduce-scatter.17.cloned.1.call-done = f32[4,32,1152]{2,1,0:T(8,128)} async-done(((f32[4,128,1152]{2,1,0:T(8,128)}), f32[4,32,1152]{2,1,0:T(8,128)}) %reduce-scatter.17.cloned.1.call-update) | async-done | bytes 589840 | tf_op jit(solution)/shard_map/reduce_scatter | solution.py:63
  579.6 16.8 %all-gather.21.cloned.1.call-done = bf16[4,128,1152]{2,1,0:T(8,128)(2,1)} async-done(((bf16[4,32,1152]{2,1,0:T(8,128)(2,1)}), bf16[4,128,1152]{2,1,0:T(8,128)(2,1)}) %all-gather.21.cloned.1.call-update) | async-done | bytes 1179664 | tf_op jit(solution)/shard_map/all_gather | solution.py:67
  605.5 32.9 %reduce-scatter.21.cloned.1.call-done = f32[4,32,1152]{2,1,0:T(8,128)} async-done(((f32[4,128,1152]{2,1,0:T(8,128)}), f32[4,32,1152]{2,1,0:T(8,128)}) %reduce-scatter.21.cloned.1.call-update) | async-done | bytes 589840 | tf_op jit(solution)/shard_map/reduce_scatter | solution.py:63
  647.0 3.8 copy.145
  650.8 4.1 reshape.274
  659.2 5.7 convolution_bitcast_fusion.1
  665.6 4.7 convolution_bitcast_fusion.2
  670.3 8.6 copy.147
  678.9 9.0 reshape.276
  694.5 5.7 fusion.44
  702.5 10.8 gather_fusion.4
  713.4 8.4 gather_fusion.2
  731.4 78.5 %scatter_fusion = bf16[4,256,1152]{2,1,0:T(8,128)(2,1)} fusion(bf16[4,256,1152]{2,1,0:T(8,128)(2,1)} %broadcast_in_dim.26, s32[512]{0:T(512)S(1)} %get-tuple-element.152, bf16[512,1152]{1,0:T(8,128)(2,1)} %bitcast.219), kind=kCustom, calls=%fused_computation.5 | custom fusion | bytes 3543040 | tf_op jit(solution)/shard_map/scatter | solution.py:59
  809.9 78.8 %scatter_fusion.1 = bf16[4,256,1152]{2,1,0:T(8,128)(2,1)} fusion(bf16[4,256,1152]{2,1,0:T(8,128)(2,1)} %scatter_fusion, s32[512]{0:T(512)S(1)} %get-tuple-element.150, bf16[512,1152]{1,0:T(8,128)(2,1)} %bitcast.207), kind=kCustom, calls=%fused_computation.6 | custom fusion | bytes 3543040 | tf_op jit(solution)/shard_map/scatter | solution.py:59
  893.6 4.0 convolution_bitcast_fusion.5
  897.7 11.4 psum.7
  909.7 55.2 %reduce-scatter.33.cloned.1.call-done = f32[144,864]{1,0:T(8,128)} async-done(((f32[1152,864]{1,0:T(8,128)}), f32[144,864]{1,0:T(8,128)}) %reduce-scatter.33.cloned.1.call-update) | async-done | bytes 497680
  979.2 11.0 all-gather.23.cloned.1.call-done
  992.7 80.0 %scatter_fusion.2 = f32[4,256,1152]{2,1,0:T(8,128)} fusion(f32[4,256,1152]{2,1,0:T(8,128)} %broadcast_in_dim.35, s32[512]{0:T(512)S(1)} %get-tuple-element.152, f32[512,1152]{1,0:T(8,128)} %bitcast.217), kind=kCustom, calls=%fused_computation.7 | custom fusion | bytes 7081984 | tf_op jit(solution)/shard_map/scatter | solution.py:59
  1072.7 79.7 %scatter_fusion.3 = f32[4,256,1152]{2,1,0:T(8,128)} fusion(f32[4,256,1152]{2,1,0:T(8,128)} %scatter_fusion.2, s32[512]{0:T(512)S(1)} %get-tuple-element.150, f32[512,1152]{1,0:T(8,128)} %bitcast.204), kind=kCustom, calls=%fused_computation.8 | custom fusion | bytes 7081984 | tf_op jit(solution)/shard_map/scatter | solution.py:59
  1152.4 21.2 %reduce-scatter.23.cloned.1.call-done = f32[144,6,288]{2,0,1:T(8,128)} async-done(((f32[1152,6,288]{2,0,1:T(8,128)}), f32[144,6,288]{2,0,1:T(8,128)}) %reduce-scatter.23.cloned.1.call-update) | async-done | bytes 995344 | tf_op jit(solution)/shard_map/reduce_scatter | solution.py:253
  1173.6 4.8 multiply_add_fusion
  (234 shorter events, 137.5 us)
Async XLA Ops:
  7.2 4.1 copy-start
  7.2 2.5 copy-start.16
  7.2 3.4 copy-start.22
  7.2 4.0 copy-start.45
  7.2 101.4 %all-gather.9.cloned.1.call-start = ((), (), s32[]{:S(2)}) async-start(), calls=%async_computation.10 | async-start | bytes 5971968 | tf_op jit(solution)/shard_map/all_gather | solution.py:101
  9.7 155.0 %all-gather.11.cloned.1.call-start = ((), (), s32[]{:S(2)}) async-start(), calls=%async_computation.11 | async-start | bytes 2985984 | tf_op jit(solution)/shard_map/all_gather | solution.py:102
  10.5 241.5 %reduce-scatter.15.cloned.1.call-start = ((), (), s32[]{:S(2)}) async-start(), calls=%async_computation.12 | async-start | bytes 2949120 | tf_op jit(solution)/shard_map/reduce_scatter | solution.py:63
  17.6 147.2 %copy-start.37 = (f32[4,128]{1,0:T(4,128)}, f32[4,128]{1,0:T(4,128)S(1)}, u32[]{:S(2)}) copy-start(f32[4,128]{1,0:T(4,128)S(1)} %broadcast_multiply_fusion.5) | copy-start | bytes 6148
  18.1 146.6 %copy-start.39 = (f32[4,128]{1,0:T(4,128)}, f32[4,128]{1,0:T(4,128)S(1)}, u32[]{:S(2)}) copy-start(f32[4,128]{1,0:T(4,128)S(1)} %add_rsqrt_fusion.1) | copy-start | bytes 6148
  172.8 99.0 %all-gather.13.cloned.1.call-start = ((), (), s32[]{:S(2)}) async-start(), calls=%async_computation.13 | async-start | bytes 1474560 | tf_op jit(solution)/shard_map/all_gather | solution.py:67
  174.7 11.3 collective-permute-start
  186.0 20.1 %collective-permute-start.1 = (bf16[144,1152]{1,0:T(8,128)(2,1)}, bf16[144,1152]{1,0:T(8,128)(2,1)}, u32[]{:S(2)}, u32[]{:S(2)}) collective-permute-start(bf16[144,1152]{1,0:T(8,128)(2,1)} %collective-permute-done), channel_id=1, source_target_pairs={{0,4},{4,8},{8,12},{12,16},{16,20},{20,24},{24,28},{28,0},{1,5},{5... | collective-permute-start | bytes 995336 | tf_op jit(solution)/shard_map/ppermute | solution.py:26
  186.0 24.4 %collective-permute-start.4 = (bf16[144,1152]{1,0:T(8,128)(2,1)}, bf16[144,1152]{1,0:T(8,128)(2,1)}, u32[]{:S(2)}, u32[]{:S(2)}) collective-permute-start(bf16[144,1152]{1,0:T(8,128)(2,1)} %convert_element_type.93), channel_id=1, source_target_pairs={{4,0},{8,4},{12,8},{16,12},{20,16},{24,20},{28,24},{0,28},{5,1},{9... | collective-permute-start | bytes 995336 | tf_op jit(solution)/shard_map/ppermute | solution.py:28
  195.0 11.1 copy-start.38
  195.0 11.1 copy-start.40
  206.1 14.9 %collective-permute-start.2 = (bf16[144,1152]{1,0:T(8,128)(2,1)}, bf16[144,1152]{1,0:T(8,128)(2,1)}, u32[]{:S(2)}, u32[]{:S(2)}) collective-permute-start(bf16[144,1152]{1,0:T(8,128)(2,1)} %collective-permute-done.1), channel_id=1, source_target_pairs={{0,4},{4,8},{8,12},{12,16},{16,20},{20,24},{24,28},{28,0},{1,5},{5... | collective-permute-start | bytes 995336 | tf_op jit(solution)/shard_map/ppermute | solution.py:26
  206.1 17.4 %copy-start.43 = (pred[4,128]{1,0:T(4,128)(4,1)S(1)}, pred[4,128]{1,0:T(4,128)(4,1)}, u32[]{:S(2)}) copy-start(pred[4,128]{1,0:T(4,128)(4,1)} %copy-done.42) | copy-start | bytes 1540
  210.4 16.5 %collective-permute-start.5 = (bf16[144,1152]{1,0:T(8,128)(2,1)}, bf16[144,1152]{1,0:T(8,128)(2,1)}, u32[]{:S(2)}, u32[]{:S(2)}) collective-permute-start(bf16[144,1152]{1,0:T(8,128)(2,1)} %collective-permute-done.4), channel_id=1, source_target_pairs={{4,0},{8,4},{12,8},{16,12},{20,16},{24,20},{28,24},{0,28},{5,1},{9... | collective-permute-start | bytes 995336 | tf_op jit(solution)/shard_map/ppermute | solution.py:28
  221.0 14.6 %collective-permute-start.3 = (bf16[144,1152]{1,0:T(8,128)(2,1)}, bf16[144,1152]{1,0:T(8,128)(2,1)}, u32[]{:S(2)}, u32[]{:S(2)}) collective-permute-start(bf16[144,1152]{1,0:T(8,128)(2,1)} %collective-permute-done.2), channel_id=1, source_target_pairs={{0,4},{4,8},{8,12},{12,16},{16,20},{20,24},{24,28},{28,0},{1,5},{5... | collective-permute-start | bytes 995336 | tf_op jit(solution)/shard_map/ppermute | solution.py:26
  226.9 33.8 %collective-permute-start.6 = (bf16[144,1152]{1,0:T(8,128)(2,1)}, bf16[144,1152]{1,0:T(8,128)(2,1)}, u32[]{:S(2)}, u32[]{:S(2)}) collective-permute-start(bf16[144,1152]{1,0:T(8,128)(2,1)} %collective-permute-done.5), channel_id=1, source_target_pairs={{4,0},{8,4},{12,8},{16,12},{20,16},{24,20},{28,24},{0,28},{5,1},{9... | collective-permute-start | bytes 995336 | tf_op jit(solution)/shard_map/ppermute | solution.py:28
  252.1 2.3 copy-start.29
  252.1 2.3 copy-start.35
  255.3 130.6 %reduce-scatter.29.cloned.1.call-start = ((), (), s32[]{:S(2)}) async-start(), calls=%async_computation.25 | async-start | bytes 5971968 | tf_op jit(solution)/shard_map/reduce_scatter | solution.py:257
  271.8 5.5 copy-start.9
  271.8 5.5 copy-start.34
  281.5 162.8 %all-gather.15.cloned.1.call-start = ((), (), s32[]{:S(2)}) async-start(), calls=%async_computation.14 | async-start | bytes 2985984 | tf_op jit(solution)/shard_map/all_gather | solution.py:105
  389.4 111.3 %all-gather.19.cloned.1.call-start = ((), (), s32[]{:S(2)}) async-start(), calls=%async_computation.17 | async-start | bytes 2985984 | tf_op jit(solution)/shard_map/all_gather | solution.py:168
  390.1 147.8 %reduce-scatter.19.cloned.1.call-start = ((), (), s32[]{:S(2)}) async-start(), calls=%async_computation.18 | async-start | bytes 2949120 | tf_op jit(solution)/shard_map/reduce_scatter | solution.py:63
  506.2 67.6 %reduce-scatter.17.cloned.1.call-start = ((), (), s32[]{:S(2)}) async-start(), calls=%async_computation.15 | async-start | bytes 2949120 | tf_op jit(solution)/shard_map/reduce_scatter | solution.py:63
  512.3 84.1 %all-gather.21.cloned.1.call-start = ((), (), s32[]{:S(2)}) async-start(), calls=%async_computation.19 | async-start | bytes 1474560 | tf_op jit(solution)/shard_map/all_gather | solution.py:67
  573.7 4.3 copy-start.31
  578.8 59.6 %reduce-scatter.21.cloned.1.call-start = ((), (), s32[]{:S(2)}) async-start(), calls=%async_computation.20 | async-start | bytes 2949120 | tf_op jit(solution)/shard_map/reduce_scatter | solution.py:63
  605.2 87.7 %reduce-scatter.31.cloned.1.call-start = ((), (), s32[]{:S(2)}) async-start(), calls=%async_computation.26 | async-start | bytes 737280
  655.0 74.8 %all-gather.17.cloned.1.call-start = ((), (), s32[]{:S(2)}) async-start(), calls=%async_computation.16 | async-start | bytes 1474560 | tf_op jit(solution)/shard_map/all_gather | solution.py:67
  655.7 233.0 %reduce-scatter.25.cloned.1.call-start = ((), (), s32[]{:S(2)}) async-start(), calls=%async_computation.23 | async-start | bytes 1990656 | tf_op jit(solution)/shard_map/reduce_scatter | solution.py:255
  659.2 231.4 %reduce-scatter.27.cloned.1.call-start = ((), (), s32[]{:S(2)}) async-start(), calls=%async_computation.24 | async-start | bytes 5971968 | tf_op jit(solution)/shard_map/reduce_scatter | solution.py:256
  665.0 299.9 %reduce-scatter.33.cloned.1.call-start = ((), (), s32[]{:S(2)}) async-start(), calls=%async_computation.27 | async-start | bytes 4644864
  687.9 6.5 copy-start.32
  688.0 302.2 %all-gather.23.cloned.1.call-start = ((), (), s32[]{:S(2)}) async-start(), calls=%async_computation.21 | async-start | bytes 2949120 | tf_op jit(solution)/shard_map/all_gather | solution.py:232
  692.3 481.3 %reduce-scatter.23.cloned.1.call-start = ((), (), s32[]{:S(2)}) async-start(), calls=%async_computation.22 | async-start | bytes 11943936 | tf_op jit(solution)/shard_map/reduce_scatter | solution.py:253
  700.2 2.3 copy-start.46
  713.4 8.4 copy-start.24
  725.4 2.7 copy-start.4
  809.9 78.8 %copy-start.23 = (f32[288,144]{0,1:T(8,128)S(1)}, f32[288,144]{0,1:T(8,128)}, u32[]{:S(2)}) copy-start(f32[288,144]{0,1:T(8,128)} %param.33) | copy-start | bytes 497668
  809.9 78.8 %copy-start.30 = (f32[288,144]{0,1:T(8,128)S(1)}, f32[288,144]{0,1:T(8,128)}, u32[]{:S(2)}) copy-start(f32[288,144]{0,1:T(8,128)} %param.43) | copy-start | bytes 497668
  809.9 80.7 %copy-start.6 = (f32[144,1152]{1,0:T(8,128)S(1)}, f32[144,1152]{1,0:T(8,128)}, u32[]{:S(2)}) copy-start(f32[144,1152]{1,0:T(8,128)} %param.34) | copy-start | bytes 1990660
  897.7 72.1 %copy-start.10 = (f32[3,144,288]{1,2,0:T(8,128)S(1)}, f32[3,144,288]{1,2,0:T(8,128)}, u32[]{:S(2)}) copy-start(f32[3,144,288]{1,2,0:T(8,128)} %copy.131) | copy-start | bytes 1492996
  973.2 4.9 copy-start.11
  (26 other events, 30.2 us)
Sparse Core Ops, SparseCore 0:
  10.9 97.6 all-gather.8
  111.4 53.2 all-gather.10
  172.9 31.6 reduce-scatter.14
  255.4 16.3 all-gather.12
  281.7 104.1 reduce-scatter.28
  389.5 54.7 all-gather.14
  447.1 53.5 all-gather.18
  506.3 31.6 reduce-scatter.18
  540.6 33.0 reduce-scatter.16
  578.9 17.4 all-gather.20
  605.3 33.0 reduce-scatter.20
  655.1 22.0 reduce-scatter.30
  679.4 17.4 all-gather.16
  700.6 66.5 reduce-scatter.24
  770.6 103.0 reduce-scatter.26
  877.5 87.3 reduce-scatter.32
  966.3 23.8 all-gather.22
  993.6 179.9 reduce-scatter.22
